TPU v7x, 256 devices: a whole 4x4x8 slice. The times are simulated.
256 devices in a mesh: group: 32 (over y_hi, z, core), tok: 8 (over x, y_lo).
Axes of the slice: x: 4, y: 4 (y_hi: 2, y_lo: 2; y = y_hi * 2 + y_lo), z: 8, core: 2. Of those that a mesh axis runs over, the one named last changes fastest.
Arguments:
- latents: bfloat16 [32768, 5120], P(('group', 'tok')), may hold values from -6 to 6
- timesteps: int32 [32], P('group'), may hold values from 0 to 999
- mod_shift: float32 [5120], replicated, may hold values from -3 to 3
- mod_scale: float32 [5120], replicated, may hold values from -1.5 to 1.5
- w_query: bfloat16 [5120, 3072], P('group', 'tok'), may hold values from -7 to 7
- w_key: bfloat16 [5120, 3072], P('group', 'tok'), may hold values from -7 to 7
- w_value: bfloat16 [5120, 3072], P('group', 'tok'), may hold values from -0.078125 to 0.078125
- query_gain: float32 [3072], P('tok'), may hold values from 0.5 to 1.5
- key_gain: float32 [3072], P('tok'), may hold values from 0.5 to 1.5
- cache_keys: bfloat16 [32768, 3072], P('group', 'tok'), may hold values from -85 to 85
- cache_values: bfloat16 [32768, 3072], P('group', 'tok'), may hold values from -6 to 6
- owners: int32 [32], replicated, may hold values from 0 to 31, each once
- tile_mask: int32 [24, 8, 24], P('tok'), may hold values from 0 to 1, as said below
Outputs:
- attended: bfloat16 [32768, 3072], P('group', 'tok')
Inputs may be any that keep to these rules, and one draw needn't show every extreme that they name: `tile_mask`: each query tile i of each head sees 1 to 8 key tiles, always tile 2 * 8 + i; some query tile sees exactly 8.
All inputs are finite; a program needn't handle non-finite values.
Results may differ from a plain program's by a relative error of at most 0.012.
The roundings to bfloat16 on the way count: a program that leaves them out, or rounds other values in their place, can miss the bound.
Values may be sent and summed in bfloat16 or wider, within the bound.
No kernel may reach another device: no remote copies, remote signals or barrier semaphores. Data moves between devices by JAX's collectives and lax.ppermute only.
A program may use at most 128 MiB of HBM per device.

v0:
```python
import math
import jax
import jax.numpy as jnp
from jax import lax
from jax.sharding import PartitionSpec as P

EPSILON = 1e-06


def from_behind(block, axis, distance):
    devices = range(lax.axis_size(axis))
    route = [(i - distance, i) for i in devices if i - distance in devices]
    return lax.ppermute(block, axis, route)


def spread_2(value, axis, source):
    kept = jnp.where(lax.axis_index(axis) == source, value, 0).astype(value.dtype)
    return lax.psum(kept, axis)


def modulate(rows_block, timestep, mod_shift, mod_scale):
    values = rows_block.astype(jnp.float32)
    width = values.shape[-1]
    centred = values - jnp.mean(values, axis=-1, keepdims=True)
    spread = jnp.mean(centred * centred, axis=-1, keepdims=True)
    normed = centred * lax.rsqrt(spread + EPSILON)
    freqs = jnp.exp(-math.log(10000.0) * jnp.arange(width, dtype=jnp.float32) / width)
    angles = timestep.astype(jnp.float32) * freqs
    return (
        normed * (1.0 + mod_scale + 0.5 * jnp.cos(angles)) + mod_shift + 0.5 * jnp.sin(angles)
    ).astype(jnp.bfloat16)


def scaled_rows(raw, squares, width, gain):
    return (raw * lax.rsqrt(squares / width + EPSILON)[:, None] * gain).astype(jnp.bfloat16)


def listed_attention(query_tiles, key_tiles, value_tiles, allowed, score_scale):
    key_tile_count = allowed.shape[2]
    active_count = jnp.sum(allowed, axis=-1)
    tile_order = jnp.argsort(1 - allowed, axis=-1, stable=True)
    visits = min(8, key_tile_count)
    tile_shape = query_tiles.shape
    tile_ids = jnp.arange(key_tile_count, dtype=jnp.int32)
    start_max = jnp.full(tile_shape[:3], -1e30, jnp.float32)
    start_sum = jnp.zeros(tile_shape[:3], jnp.float32)
    start_acc = jnp.zeros(tile_shape, jnp.float32)

    def visit(visit_index, carry):
        running_max, running_sum, accumulated = carry
        picked = lax.dynamic_index_in_dim(tile_order, visit_index, 2, keepdims=False)
        selector = (picked[:, :, None] == tile_ids[None, None, :]).astype(jnp.bfloat16)
        key_tile = jnp.einsum(
            "hqk,hkjd->hqjd", selector, key_tiles, preferred_element_type=jnp.float32
        ).astype(jnp.bfloat16)
        value_tile = jnp.einsum(
            "hqk,hkjd->hqjd", selector, value_tiles, preferred_element_type=jnp.float32
        ).astype(jnp.bfloat16)
        scores = (
            jnp.einsum("hqid,hqjd->hqij", query_tiles, key_tile, preferred_element_type=jnp.float32)
            * score_scale
        )
        is_live = (visit_index < active_count)[:, :, None]
        new_max = jnp.where(
            is_live, jnp.maximum(running_max, jnp.max(scores, axis=-1)), running_max
        )
        shrink = jnp.exp(running_max - new_max)
        weights = jnp.exp(scores - new_max[..., None])
        new_sum = jnp.where(is_live, running_sum * shrink + jnp.sum(weights, axis=-1), running_sum)
        added = jnp.einsum(
            "hqij,hqjd->hqid",
            weights.astype(jnp.bfloat16),
            value_tile,
            preferred_element_type=jnp.float32,
        )
        new_acc = jnp.where(
            is_live[..., None], accumulated * shrink[..., None] + added, accumulated
        )
        return (new_max, new_sum, new_acc)

    final_max, final_sum, final_acc = lax.fori_loop(
        0, visits, visit, (start_max, start_sum, start_acc)
    )
    return (final_acc / final_sum[..., None]).astype(jnp.bfloat16)


def local(
    latents,
    timesteps,
    mod_shift,
    mod_scale,
    w_query,
    w_key,
    w_value,
    query_gain,
    key_gain,
    cache_keys,
    cache_values,
    owners,
    tile_mask,
):
    modulated = modulate(latents, timesteps[0], mod_shift, mod_scale)
    root = owners[owners.shape[0] - 1]
    head_cols = w_query.shape[1]
    slabs = (
        lax.all_gather(w_query, "group", axis=0, tiled=True),
        lax.all_gather(w_key, "group", axis=0, tiled=True),
        lax.all_gather(w_value, "group", axis=0, tiled=True),
    )
    joined = jnp.concatenate(slabs, axis=1)
    projected = jnp.dot(
        lax.all_gather(modulated, "tok", axis=0, tiled=True),
        joined,
        preferred_element_type=jnp.float32,
    )
    raw_query = projected[:, :head_cols]
    raw_key = projected[:, head_cols : 2 * head_cols]
    raw_value = projected[:, 2 * head_cols :]
    query_squares, key_squares = lax.psum(
        (jnp.sum(raw_query * raw_query, axis=1), jnp.sum(raw_key * raw_key, axis=1)), "tok"
    )
    width = head_cols * lax.axis_size("tok")
    query_rows = scaled_rows(raw_query, query_squares, width, query_gain)
    key_rows = scaled_rows(raw_key, key_squares, width, key_gain)
    value_rows = raw_value.astype(jnp.bfloat16)
    earlier_keys, earlier_values = from_behind((key_rows, value_rows), "group", 1)
    cached = (spread_2(cache_keys, "group", root), spread_2(cache_values, "group", root))
    group_rows = query_rows.shape[0]
    local_heads = tile_mask.shape[0]
    query_tiles = tile_mask.shape[1]
    key_tile_count = tile_mask.shape[2]
    tile_rows = group_rows // query_tiles
    head_size = head_cols // local_heads
    score_scale = 1.0 / math.sqrt(head_size)
    context_keys = jnp.concatenate([cached[0], earlier_keys, key_rows], axis=0)
    context_values = jnp.concatenate([cached[1], earlier_values, value_rows], axis=0)
    is_first = lax.axis_index("group") == 0
    tile_ids = jnp.arange(key_tile_count, dtype=jnp.int32)
    earlier_region = (tile_ids >= query_tiles) & (tile_ids < 2 * query_tiles)
    allowed = jnp.where(earlier_region[None, None, :] & is_first, 0, tile_mask)
    query_heads = query_rows.reshape(group_rows, local_heads, head_size).transpose(1, 0, 2)
    key_heads = context_keys.reshape(3 * group_rows, local_heads, head_size).transpose(1, 0, 2)
    value_heads = context_values.reshape(3 * group_rows, local_heads, head_size).transpose(1, 0, 2)
    attended = listed_attention(
        query_heads.reshape(local_heads, query_tiles, tile_rows, head_size),
        key_heads.reshape(local_heads, key_tile_count, tile_rows, head_size),
        value_heads.reshape(local_heads, key_tile_count, tile_rows, head_size),
        allowed,
        score_scale,
    ).reshape(local_heads, group_rows, head_size)
    return attended.transpose(1, 0, 2).reshape(group_rows, head_cols)


def solution(mesh):
    return jax.shard_map(
        local,
        mesh=mesh,
        in_specs=(
            P(("group", "tok"), None),
            P("group"),
            P(),
            P(),
            P("group", "tok"),
            P("group", "tok"),
            P("group", "tok"),
            P("tok"),
            P("tok"),
            P("group", "tok"),
            P("group", "tok"),
            P(),
            P("tok", None, None),
        ),
        out_specs=P("group", "tok"),
        check_vma=False,
    )
```

profile of v0, /device:TPU:1, one launch (start us, length us, event | category | flops | bytes accessed | tf_op | source)
XLA Modules:
  0.0 861.7 jit_solution(1480350413721025981)
XLA Ops:
  9.4 1.6 convert_reduce_fusion
  11.7 1.7 fusion.28
  14.8 1.4 broadcast_select_fusion
  16.2 83.9 %all-gather.11.cloned.1.call-done = bf16[5120,384]{1,0:T(8,128)(2,1)} async-done(((bf16[160,384]{1,0:T(8,128)(2,1)}), bf16[5120,384]{1,0:T(8,128)(2,1)}) %all-gather.11.cloned.1.call-update) | async-done | bytes 3932176 | tf_op jit(solution)/shard_map/all_gather | solution.py:108
  100.1 85.2 %all-gather.7.cloned.1.call-done = bf16[5120,384]{1,0:T(8,128)(2,1)} async-done(((bf16[160,384]{1,0:T(8,128)(2,1)}), bf16[5120,384]{1,0:T(8,128)(2,1)}) %all-gather.7.cloned.1.call-update) | async-done | bytes 3932176 | tf_op jit(solution)/shard_map/all_gather | solution.py:106
  185.3 85.3 %all-gather.9.cloned.1.call-done = bf16[5120,384]{1,0:T(8,128)(2,1)} async-done(((bf16[160,384]{1,0:T(8,128)(2,1)}), bf16[5120,384]{1,0:T(8,128)(2,1)}) %all-gather.9.cloned.1.call-update) | async-done | bytes 3932176 | tf_op jit(solution)/shard_map/all_gather | solution.py:107
  270.6 208.0 %all-gather.5.cloned.1.call-done = bf16[1024,5120]{1,0:T(8,128)(2,1)} async-done(((bf16[128,5120]{1,0:T(8,128)(2,1)}), bf16[1024,5120]{1,0:T(8,128)(2,1)}) %all-gather.5.cloned.1.call-update) | async-done | bytes 10485776 | tf_op jit(solution)/shard_map/all_gather | solution.py:112
  478.6 24.9 %fusion.16 = f32[1024,1152]{1,0:T(8,128)S(1)} fusion(bf16[1024,5120]{1,0:T(8,128)(2,1)} %all-gather.5.cloned.1.call-done, bf16[5120,384]{1,0:T(8,128)(2,1)} %all-gather.11.cloned.1.call-done, bf16[5120,384]{1,0:T(8,128)(2,1)} %all-gather.9.cloned.1.call-done, bf16[5120,384]{1,0:T(8,128)(2,1)} %all-gather.7.cloned.1.call-done), kind=kOutput, calls=%fused_computation.25 | convolution fusion | flops 12114984960 | bytes 27000832 | tf_op jit(solution)/shard_map/dot_general | solution.py:111
  503.4 2.1 copy-done.2
  505.9 16.9 %all-reduce = (f32[1024]{0:T(1024)S(1)}, f32[1024]{0:T(1024)S(1)}) all-reduce(f32[1024]{0:T(1024)S(1)} %get-tuple-element.221, f32[1024]{0:T(1024)S(1)} %get-tuple-element.220), channel_id=1, replica_groups=mesh['group'=32,'tok'=8] {'tok'}, use_global_device_ids=true, to_apply=%region_5.0 | all-reduce | flops 2048 | bytes 16384 | tf_op jit(solution)/shard_map/psum | solution.py:119
  522.9 3.4 multiply_convert_fusion
  526.3 6.9 collective-permute-start
  533.1 1.5 slice.25
  534.6 2.1 collective-permute-start.1
  537.0 1.6 sort.17
  538.6 1.4 copy.22
  540.0 1.2 copy.37
  541.2 215.3 %all-reduce.4.cloned.1.call-done = (bf16[1024,384]{1,0:T(8,128)(2,1)}, bf16[1024,384]{1,0:T(8,128)(2,1)}) async-done(((bf16[1024,384]{1,0:T(8,128)(2,1)}, bf16[1024,384]{1,0:T(8,128)(2,1)}), (bf16[1024,384]{1,0:T(8,128)(2,1)}, bf16[1024,384]{1,0:T(8,128)(2,1)})) %all-reduce.4.cloned.1.call-update) | async-done | bytes 1572880 | tf_op jit(solution)/shard_map/psum | solution.py:18
  756.5 3.3 pad_maximum_fusion
  759.7 4.3 copy.21
  764.0 4.4 copy.36
  768.4 2.8 pad_maximum_fusion.1
  771.1 4.3 copy.23
  775.4 4.3 copy.38
  779.7 73.5 %while.18 = (s32[]{:T(128)}, f32[3,8,128]{2,1,0:T(8,128)S(1)}, f32[3,8,128]{2,1,0:T(8,128)S(1)}, f32[3,8,128,128]{3,2,1,0:T(8,128)S(1)}, s32[3,8]{1,0:T(4,128)S(...) while((s32[]{:T(128)}, f32[3,8,128]{2,1,0:T(8,128)S(1)}, ...), condition=%wide.region_13.14_spmd.clone, body=%wide.region_10.13_spmd.clone.sunk | while | flops 243030176 | bytes 19858332 | solution.py:81
  779.7 3.5 fusion.47
  784.3 3.4 fusion.49
  787.8 1.1 add_select_fusion.5
  788.9 3.5 fusion.47
  793.5 3.4 fusion.49
  796.9 1.1 add_select_fusion.5
  798.1 3.5 fusion.47
  802.7 3.4 fusion.49
  806.1 1.1 add_select_fusion.5
  807.3 3.5 fusion.47
  811.9 3.4 fusion.49
  816.5 3.5 fusion.47
  821.1 3.4 fusion.49
  824.5 1.1 add_select_fusion.5
  825.7 3.5 fusion.47
  830.3 3.4 fusion.49
  833.7 1.1 add_select_fusion.5
  834.9 3.5 fusion.47
  839.5 3.4 fusion.49
  842.9 1.1 add_select_fusion.5
  844.1 3.5 fusion.47
  848.7 3.4 fusion.49
  854.0 1.2 copy.29
  (132 shorter events, 16.2 us)
Async XLA Ops:
  6.5 4.5 copy-start.1
  6.5 5.0 copy-start.7
  6.5 5.2 copy-start.6
  6.5 93.5 %all-gather.11.cloned.1.call-start = ((), (), s32[]{:S(2)}) async-start(), calls=%async_computation.3 | async-start | bytes 4055040 | tf_op jit(solution)/shard_map/all_gather | solution.py:108
  7.3 178.0 %all-gather.7.cloned.1.call-start = ((), (), s32[]{:S(2)}) async-start(), calls=%async_computation.1 | async-start | bytes 4055040 | tf_op jit(solution)/shard_map/all_gather | solution.py:106
  8.0 262.5 %all-gather.9.cloned.1.call-start = ((), (), s32[]{:S(2)}) async-start(), calls=%async_computation.2 | async-start | bytes 4055040 | tf_op jit(solution)/shard_map/all_gather | solution.py:107
  8.7 469.8 %all-gather.5.cloned.1.call-start = ((), (), s32[]{:S(2)}) async-start(), calls=%async_computation | async-start | bytes 11796480 | tf_op jit(solution)/shard_map/all_gather | solution.py:112
  11.5 2.0 copy-start.11
  11.5 3.2 copy-start.4
  11.6 3.2 copy-start.5
  13.5 743.0 %all-reduce.4.cloned.1.call-start = ((), (), s32[]{:S(2)}) async-start(), calls=%async_computation.4 | async-start | bytes 3145728 | tf_op jit(solution)/shard_map/psum | solution.py:18
  503.4 2.1 copy-start.2
  505.6 17.3 %copy-start.9 = (f32[384]{0:T(512)S(1)}, f32[384]{0:T(512)}, u32[]{:S(2)}) copy-start(f32[384]{0:T(512)} %param.22) | copy-start | bytes 4612
  505.6 17.3 %copy-start.10 = (f32[384]{0:T(512)S(1)}, f32[384]{0:T(512)}, u32[]{:S(2)}) copy-start(f32[384]{0:T(512)} %param.23) | copy-start | bytes 4612
  522.8 14.0 %copy-start.8 = (s32[3,8,24]{2,1,0:T(8,128)S(1)}, s32[3,8,24]{2,1,0:T(8,128)}, u32[]{:S(2)}) copy-start(s32[3,8,24]{2,1,0:T(8,128)} %param.27) | copy-start | bytes 6916
  526.3 230.2 %collective-permute-start = (bf16[1024,384]{1,0:T(8,128)(2,1)}, bf16[1024,384]{1,0:T(8,128)(2,1)}, u32[]{:S(2)}, u32[]{:S(2)}) collective-permute-start(bf16[1024,384]{1,0:T(8,128)(2,1)} %get-tuple-element.249), channel_id=1, source_target_pairs={{0,8},{8,16},{16,24},{24,32},{32,40},{40,48},{48,56},{56,64},{64,7... | collective-permute-start | bytes 2359304 | tf_op jit(solution)/shard_map/ppermute | solution.py:13
  534.6 233.7 %collective-permute-start.1 = (bf16[1024,384]{1,0:T(8,128)(2,1)S(1)}, bf16[1024,384]{1,0:T(8,128)(2,1)}, u32[]{:S(2)}, u32[]{:S(2)}) collective-permute-start(bf16[1024,384]{1,0:T(8,128)(2,1)S(1)} %slice.25), channel_id=1, source_target_pairs={{0,8},{8,16},{16,24},{24,32},{32,40},{40,48},{48,56},{56,64},{64,7... | collective-permute-start | bytes 2359304 | tf_op jit(solution)/shard_map/ppermute | solution.py:13
  764.0 4.4 copy-start.3
  779.7 3.5 copy-start
  788.9 3.5 copy-start
  798.1 3.5 copy-start
  807.3 3.5 copy-start
  816.5 3.5 copy-start
  825.7 3.5 copy-start
  834.9 3.5 copy-start
  844.0 3.5 copy-start
Sparse Core Ops, SparseCore 0:
  10.1 89.9 all-gather.10
  102.8 82.4 all-gather.6
  188.1 82.4 all-gather.8
  272.2 206.3 all-gather.4
  481.1 275.3 all-reduce.3
where the time goes:
time: 863 us; the launch traced here: 862 us
  waiting for transfers between devices  680 us (79%)
  matrix products  94 us (11%)
  local copies, waits for them, and re-layouts  25.7 us (3%)
  other arithmetic  20.9 us (2%)
  blocking collectives  16.9 us (2%)
  between operations  14.7 us (2%)
  starting transfers between devices  9.15 us (1%)
    psum x1, waiting for transfers between devices, spread_2(): return lax.psum(kept, axis)  215 us
    all_gather x1, waiting for transfers between devices, local(): lax.all_gather(modulated, 'tok', axis=0, tiled=True)  208 us
    all_gather x1, waiting for transfers between devices, local(): lax.all_gather(w_key, 'group', axis=0, tiled=True)  85.3 us
    all_gather x1, waiting for transfers between devices, local(): lax.all_gather(w_query, 'group', axis=0, tiled=True)  85.2 us
    all_gather x1, waiting for transfers between devices, local(): lax.all_gather(w_value, 'group', axis=0, tiled=True)  83.9 us
    dot_general x8, matrix products, visit(): jnp.einsum('hqk,hkjd->hqjd', selector, key_tiles, preferred_element_type=...  27.8 us
    dot_general x8, matrix products, visit(): jnp.einsum('hqk,hkjd->hqjd', selector, value_tiles, preferred_element_typ...  27.3 us
    dot_general x1, matrix products, local(): jnp.dot(lax.all_gather(modulated, 'tok', axis=0, tiled=True), joined, pre...  24.9 us
  transfers between devices with their start and end apart: 7, of which 5 were waited for; matrix products, arithmetic and copies ran while one was open for 6% of the time, Pallas kernels for 0%

commit v1 on v0

--- a/solution.py
+++ b/solution.py
@@ -5,6 +5,12 @@
 from jax.sharding import PartitionSpec as P
 
 EPSILON = 1e-06
+
+
+def summed_here(x, name):
+    shards = lax.all_gather(x, name, axis=0, tiled=False)
+    result = shards.sum(axis=0)
+    return result
 
 
 def from_behind(block, axis, distance):
@@ -15,7 +21,7 @@
 
 def spread_2(value, axis, source):
     kept = jnp.where(lax.axis_index(axis) == source, value, 0).astype(value.dtype)
-    return lax.psum(kept, axis)
+    return summed_here(kept, axis)
 
 
 def modulate(rows_block, timestep, mod_shift, mod_scale):

time: 863 us -> 957 us (1.11)
  waiting for transfers between devices: 680 us -> 747 us
  other arithmetic: 20.9 us -> 47.3 us
    all_gather x0 -> x2, waiting for transfers between devices: none -> 283 us  [summed_here(): shards = lax.all_gather(x, name, axis=0, tiled=False)]
    psum x1 -> x0, waiting for transfers between devices: 215 us -> none  [spread_2(): return lax.psum(kept, axis)]
    reduce_sum x0 -> x2, other arithmetic: none -> 25.8 us  [summed_here(): result = shards.sum(axis=0)]
  transfers between devices with their start and end apart: 7 -> 8, of which waited for: 5 -> 6; matrix products, arithmetic and copies ran while one was open for 6% -> 8% of each run, Pallas kernels for 0% -> 0%
where the time goes in v1:
time: 957 us; the launch traced here: 956 us
  waiting for transfers between devices  747 us (78%)
  matrix products  94 us (10%)
  other arithmetic  47.3 us (5%)
  local copies, waits for them, and re-layouts  25.7 us (3%)
  blocking collectives  16.8 us (2%)
  between operations  15 us (2%)
    all_gather x2, waiting for transfers between devices, summed_here(): shards = lax.all_gather(x, name, axis=0, tiled=False)  283 us
    all_gather x1, waiting for transfers between devices, local(): lax.all_gather(modulated, 'tok', axis=0, tiled=True)  208 us
    all_gather x1, waiting for transfers between devices, local(): lax.all_gather(w_value, 'group', axis=0, tiled=True)  85.3 us
    all_gather x1, waiting for transfers between devices, local(): lax.all_gather(w_key, 'group', axis=0, tiled=True)  85.2 us
    all_gather x1, waiting for transfers between devices, local(): lax.all_gather(w_query, 'group', axis=0, tiled=True)  83.2 us
    dot_general x8, matrix products, visit(): jnp.einsum('hqk,hkjd->hqjd', selector, key_tiles, preferred_element_type=...  27.8 us
    dot_general x8, matrix products, visit(): jnp.einsum('hqk,hkjd->hqjd', selector, value_tiles, preferred_element_typ...  27.3 us
    reduce_sum x2, other arithmetic, summed_here(): result = shards.sum(axis=0)  25.8 us
  transfers between devices with their start and end apart: 8, of which 6 were waited for; matrix products, arithmetic and copies ran while one was open for 8% of the time, Pallas kernels for 0%

profile of v1, /device:TPU:1, one launch (start us, length us, event | category | flops | bytes accessed | tf_op | source)
XLA Modules:
  0.0 955.6 jit_solution(2095208065799062583)
XLA Ops:
  9.4 1.6 convert_reduce_fusion
  11.7 1.7 fusion.28
  16.8 83.2 %all-gather.11.cloned.1.call-done = bf16[5120,384]{1,0:T(8,128)(2,1)} async-done(((bf16[160,384]{1,0:T(8,128)(2,1)}), bf16[5120,384]{1,0:T(8,128)(2,1)}) %all-gather.11.cloned.1.call-update) | async-done | bytes 3932176 | tf_op jit(solution)/shard_map/all_gather | solution.py:112
  100.1 85.2 %all-gather.13.cloned.1.call-done = bf16[5120,384]{1,0:T(8,128)(2,1)} async-done(((bf16[160,384]{1,0:T(8,128)(2,1)}), bf16[5120,384]{1,0:T(8,128)(2,1)}) %all-gather.13.cloned.1.call-update) | async-done | bytes 3932176 | tf_op jit(solution)/shard_map/all_gather | solution.py:113
  185.3 85.3 %all-gather.15.cloned.1.call-done = bf16[5120,384]{1,0:T(8,128)(2,1)} async-done(((bf16[160,384]{1,0:T(8,128)(2,1)}), bf16[5120,384]{1,0:T(8,128)(2,1)}) %all-gather.15.cloned.1.call-update) | async-done | bytes 3932176 | tf_op jit(solution)/shard_map/all_gather | solution.py:114
  270.6 208.0 %all-gather.9.cloned.1.call-done = bf16[1024,5120]{1,0:T(8,128)(2,1)} async-done(((bf16[128,5120]{1,0:T(8,128)(2,1)}), bf16[1024,5120]{1,0:T(8,128)(2,1)}) %all-gather.9.cloned.1.call-update) | async-done | bytes 10485776 | tf_op jit(solution)/shard_map/all_gather | solution.py:118
  478.6 24.9 %fusion.16 = f32[1024,1152]{1,0:T(8,128)S(1)} fusion(bf16[1024,5120]{1,0:T(8,128)(2,1)} %all-gather.9.cloned.1.call-done, bf16[5120,384]{1,0:T(8,128)(2,1)} %all-gather.15.cloned.1.call-done, bf16[5120,384]{1,0:T(8,128)(2,1)} %all-gather.13.cloned.1.call-done, bf16[5120,384]{1,0:T(8,128)(2,1)} %all-gather.11.cloned.1.call-done), kind=kOutput, calls=%fused_computation.25 | convolution fusion | flops 12114984960 | bytes 27000832 | tf_op jit(solution)/shard_map/dot_general | solution.py:117
  503.4 2.2 copy-done.2
  506.0 16.8 %all-reduce = (f32[1024]{0:T(1024)S(1)}, f32[1024]{0:T(1024)S(1)}) all-reduce(f32[1024]{0:T(1024)S(1)} %get-tuple-element.221, f32[1024]{0:T(1024)S(1)} %get-tuple-element.220), channel_id=1, replica_groups=mesh['group'=32,'tok'=8] {'tok'}, use_global_device_ids=true, to_apply=%region_5.0 | all-reduce | flops 2048 | bytes 16384 | tf_op jit(solution)/shard_map/psum | solution.py:125
  522.8 3.4 multiply_convert_fusion
  526.3 7.0 collective-permute-start
  533.3 1.5 slice.25
  534.8 2.1 collective-permute-start.1
  537.1 1.6 sort.17
  538.7 1.4 copy.22
  540.1 1.2 copy.37
  541.3 125.2 %all-gather.17.cloned.1.call-done = bf16[32768,384]{1,0:T(8,128)(2,1)} async-done(((bf16[1024,384]{1,0:T(8,128)(2,1)}), bf16[32768,384]{1,0:T(8,128)(2,1)}) %all-gather.17.cloned.1.call-update) | async-done | bytes 25165840 | tf_op jit(solution)/shard_map/all_gather | solution.py:11
  666.5 12.9 %reduce_sum.83 = bf16[1024,384]{1,0:T(8,128)(2,1)S(1)} reduce(bf16[32,1024,384]{2,1,0:T(8,128)(2,1)} %bitcast.58, bf16[]{:T(256)} %constant.80.clone.1), dimensions={0}, to_apply=%region_1.0 | reduce | flops 12189696 | bytes 25952258 | tf_op jit(solution)/shard_map/reduce_sum | solution.py:12
  679.4 3.2 pad_maximum_fusion
  682.6 4.3 copy.21
  686.9 4.3 copy.36
  691.2 157.8 %all-gather.19.cloned.1.call-done = bf16[32768,384]{1,0:T(8,128)(2,1)} async-done(((bf16[1024,384]{1,0:T(8,128)(2,1)}), bf16[32768,384]{1,0:T(8,128)(2,1)}) %all-gather.19.cloned.1.call-update) | async-done | bytes 25165840 | tf_op jit(solution)/shard_map/all_gather | solution.py:11
  849.0 12.9 %reduce_sum.88 = bf16[1024,384]{1,0:T(8,128)(2,1)S(1)} reduce(bf16[32,1024,384]{2,1,0:T(8,128)(2,1)} %bitcast.57, bf16[]{:T(256)} %constant.80.clone.1), dimensions={0}, to_apply=%region_6.7 | reduce | flops 12189696 | bytes 25952258 | tf_op jit(solution)/shard_map/reduce_sum | solution.py:12
  862.0 2.8 pad_maximum_fusion.1
  864.8 4.3 copy.23
  869.0 4.3 copy.38
  873.3 73.5 %while.18 = (s32[]{:T(128)}, f32[3,8,128]{2,1,0:T(8,128)S(1)}, f32[3,8,128]{2,1,0:T(8,128)S(1)}, f32[3,8,128,128]{3,2,1,0:T(8,128)S(1)}, s32[3,8]{1,0:T(4,128)S(...) while((s32[]{:T(128)}, f32[3,8,128]{2,1,0:T(8,128)S(1)}, ...), condition=%wide.region_13.14_spmd.clone, body=%wide.region_10.13_spmd.clone.sunk | while | flops 243030176 | bytes 19858332 | solution.py:87
  873.3 3.5 fusion.47
  878.0 3.4 fusion.49
  882.5 3.5 fusion.47
  887.2 3.4 fusion.49
  891.7 3.5 fusion.47
  896.4 3.4 fusion.49
  900.9 3.5 fusion.47
  905.5 3.4 fusion.49
  909.0 1.1 add_select_fusion.5
  910.1 3.5 fusion.47
  914.7 3.4 fusion.49
  918.2 1.1 add_select_fusion.5
  919.3 3.5 fusion.47
  923.9 3.4 fusion.49
  927.3 1.1 add_select_fusion.5
  928.5 3.5 fusion.47
  933.1 3.4 fusion.49
  937.7 3.5 fusion.47
  942.3 3.4 fusion.49
  945.7 1.1 add_select_fusion.5
  947.6 1.2 copy.29
  (136 shorter events, 20.4 us)
Async XLA Ops:
  6.5 4.5 copy-start.1
  6.5 5.0 copy-start.6
  6.5 5.2 copy-start.5
  6.5 93.5 %all-gather.11.cloned.1.call-start = ((), (), s32[]{:S(2)}) async-start(), calls=%async_computation.1 | async-start | bytes 4055040 | tf_op jit(solution)/shard_map/all_gather | solution.py:112
  7.3 178.0 %all-gather.13.cloned.1.call-start = ((), (), s32[]{:S(2)}) async-start(), calls=%async_computation.2 | async-start | bytes 4055040 | tf_op jit(solution)/shard_map/all_gather | solution.py:113
  8.0 262.5 %all-gather.15.cloned.1.call-start = ((), (), s32[]{:S(2)}) async-start(), calls=%async_computation.3 | async-start | bytes 4055040 | tf_op jit(solution)/shard_map/all_gather | solution.py:114
  8.7 469.8 %all-gather.9.cloned.1.call-start = ((), (), s32[]{:S(2)}) async-start(), calls=%async_computation | async-start | bytes 11796480 | tf_op jit(solution)/shard_map/all_gather | solution.py:118
  11.5 2.0 copy-start.10
  11.5 3.2 copy-start.3
  13.4 2.4 copy-start.4
  13.5 653.0 %all-gather.17.cloned.1.call-start = ((), (), s32[]{:S(2)}) async-start(), calls=%async_computation.4 | async-start | bytes 25952256 | tf_op jit(solution)/shard_map/all_gather | solution.py:11
  15.8 833.3 %all-gather.19.cloned.1.call-start = ((), (), s32[]{:S(2)}) async-start(), calls=%async_computation.5 | async-start | bytes 25952256 | tf_op jit(solution)/shard_map/all_gather | solution.py:11
  503.4 2.2 copy-start.2
  505.6 17.2 %copy-start.8 = (f32[384]{0:T(512)S(1)}, f32[384]{0:T(512)}, u32[]{:S(2)}) copy-start(f32[384]{0:T(512)} %param.22) | copy-start | bytes 4612
  505.6 17.2 %copy-start.9 = (f32[384]{0:T(512)S(1)}, f32[384]{0:T(512)}, u32[]{:S(2)}) copy-start(f32[384]{0:T(512)} %param.23) | copy-start | bytes 4612
  522.8 14.1 %copy-start.7 = (s32[3,8,24]{2,1,0:T(8,128)S(1)}, s32[3,8,24]{2,1,0:T(8,128)}, u32[]{:S(2)}) copy-start(s32[3,8,24]{2,1,0:T(8,128)} %param.27) | copy-start | bytes 6916
  526.3 153.2 %collective-permute-start = (bf16[1024,384]{1,0:T(8,128)(2,1)}, bf16[1024,384]{1,0:T(8,128)(2,1)}, u32[]{:S(2)}, u32[]{:S(2)}) collective-permute-start(bf16[1024,384]{1,0:T(8,128)(2,1)} %get-tuple-element.247), channel_id=1, source_target_pairs={{0,8},{8,16},{16,24},{24,32},{32,40},{40,48},{48,56},{56,64},{64,7... | collective-permute-start | bytes 2359304 | tf_op jit(solution)/shard_map/ppermute | solution.py:19
  534.8 327.2 %collective-permute-start.1 = (bf16[1024,384]{1,0:T(8,128)(2,1)S(1)}, bf16[1024,384]{1,0:T(8,128)(2,1)}, u32[]{:S(2)}, u32[]{:S(2)}) collective-permute-start(bf16[1024,384]{1,0:T(8,128)(2,1)S(1)} %slice.25), channel_id=1, source_target_pairs={{0,8},{8,16},{16,24},{24,32},{32,40},{40,48},{48,56},{56,64},{64,7... | collective-permute-start | bytes 2359304 | tf_op jit(solution)/shard_map/ppermute | solution.py:19
  873.3 3.5 copy-start
  882.5 3.5 copy-start
  891.7 3.5 copy-start
  900.9 3.5 copy-start
  910.1 3.5 copy-start
  919.3 3.5 copy-start
  928.5 3.5 copy-start
  937.7 3.5 copy-start
Sparse Core Ops, SparseCore 0:
  10.1 89.9 all-gather.10
  102.8 82.4 all-gather.12
  188.1 82.4 all-gather.14
  272.2 206.3 all-gather.8
  481.2 185.2 all-gather.16
  669.1 179.8 all-gather.18
